TPU v7x, 256 devices: a whole 4x4x8 slice. The times are simulated.
256 devices in a mesh: sec: 16 (over z, core), term: 16 (over y, x).
Axes of the slice: x: 4, y: 4, z: 8, core: 2. Of those that a mesh axis runs over, the one named last changes fastest.
Arguments:
- psi: bfloat16 [16, 512, 512], P('sec'), may hold values from -6 to 6
- left_ops: bfloat16 [16, 96, 512, 512], P('sec', 'term'), may hold values from -0.078125 to 0.078125
- right_ops: bfloat16 [16, 96, 512, 512], P('sec', 'term'), may hold values from -0.078125 to 0.078125
- term_mask: int32 [16, 96], P('sec', 'term'), may hold values 0 or 1
- pair_src: int32 [16], P('sec'), may hold values from 0 to 15, each once
- pair_dst: int32 [16], P('sec'), may hold values from 0 to 15, each once
Outputs:
- sigma: bfloat16 [16, 512, 512], P('sec')
Inputs may be any that keep to these rules, and one draw needn't show every extreme that they name: `pair_src`: each of the 16 sector blocks is the source of exactly one pair. `pair_dst`: each of the 16 sector blocks is the target of exactly one pair.
All inputs are finite; a program needn't handle non-finite values. No bound on the sum of `term_mask` on one device may be relied on, other than what follows from the above.
Results may differ from a plain program's by a relative error of at most 0.0065.
Values may be sent and summed in bfloat16 or wider, within the bound.
A program may use at most 64 MiB of HBM per device.

v0:
```python
import jax
import jax.numpy as jnp
from jax import lax
from jax.sharding import PartitionSpec as P


def in_blocks(value, dim, peers):
    shape = value.shape
    pieces = value.reshape(*shape[:dim], peers, shape[dim] // peers, *shape[dim + 1 :])
    return jnp.moveaxis(pieces, dim, 0)


def sent_and_summed(value, axis, dim):
    pieces = in_blocks(value, dim, lax.axis_size(axis))
    arrived = lax.all_to_all(pieces, axis, split_axis=0, concat_axis=0, tiled=True)
    return arrived.astype(jnp.float32).sum(axis=0)


def in_one_piece(arrays, axis, dim, along):
    columns = [a.reshape(*a.shape[:along], -1) for a in arrays]
    both = jnp.concatenate(columns, axis=along)
    filled, at, finished = (lax.all_gather(both, axis, axis=dim, tiled=True), 0, [])
    for a, column in zip(arrays, columns):
        piece = filled[..., at : at + column.shape[along]]
        finished.append(piece.reshape(*piece.shape[:along], *a.shape[along:]))
        at += column.shape[along]
    return tuple(finished)


def in_order(pieces, dim):
    pieces = jnp.moveaxis(pieces, 0, dim)
    shape = pieces.shape
    return pieces.reshape(*shape[:dim], shape[dim] * shape[dim + 1], *shape[dim + 2 :])


def copy_for_each(value, axis):
    peers = lax.axis_size(axis)
    return lax.all_to_all(
        jnp.broadcast_to(value[None], (peers, *value.shape)), axis, 0, 0, tiled=True
    )


def gathered_copies(value, axis, dim):
    return in_order(copy_for_each(value, axis), dim)


def local(psi, left_ops, right_ops, term_mask, pair_src, pair_dst):
    whole = lax.all_gather(psi, "sec", axis=0, tiled=True)
    order = psi.shape[1]
    local_pairs = psi.shape[0]
    local_terms = left_ops.shape[1]
    zero_block = jnp.zeros((order, order), jnp.float32)
    source = pair_src[0]
    target = pair_dst[0]
    src_block = lax.dynamic_index_in_dim(whole, source, 0, keepdims=False)
    dst_block = lax.dynamic_index_in_dim(whole, target, 0, keepdims=False)

    def term_step(acc, term):

        def active(carry):
            fwd_acc, adj_acc = carry
            left = left_ops[0, term]
            right = right_ops[0, term]
            inner_fwd = jnp.dot(left, src_block, preferred_element_type=jnp.float32).astype(
                jnp.bfloat16
            )
            inner_adj = jnp.dot(left.T, dst_block, preferred_element_type=jnp.float32).astype(
                jnp.bfloat16
            )
            fwd_acc = fwd_acc + jnp.dot(inner_fwd, right.T, preferred_element_type=jnp.float32)
            adj_acc = adj_acc + jnp.dot(inner_adj, right, preferred_element_type=jnp.float32)
            return (fwd_acc, adj_acc)

        return (lax.cond(term_mask[0, term] == 1, active, lambda carry: carry, acc), None)

    (fwd, adj), _ = lax.scan(
        term_step, (zero_block, zero_block), jnp.arange(local_terms, dtype=jnp.int32)
    )
    fwd_list = [fwd]
    adj_list = [adj]
    stacked = jnp.stack([jnp.stack(fwd_list), jnp.stack(adj_list)], axis=1)
    pieces = sent_and_summed(stacked.astype(jnp.bfloat16), "term", 2)
    all_pieces, all_src, all_dst = in_one_piece(
        (pieces, pair_src.astype(jnp.float32), pair_dst.astype(jnp.float32)), "sec", 0, 1
    )
    mine = (lax.axis_index("sec") * local_pairs + jnp.arange(local_pairs, dtype=jnp.int32)).astype(
        jnp.float32
    )
    pick_fwd = (all_dst[None, :] == mine[:, None]).astype(jnp.float32)
    pick_adj = (all_src[None, :] == mine[:, None]).astype(jnp.float32)
    rows_fwd = jnp.einsum(
        "sk,krc->src", pick_fwd, all_pieces[:, 0], precision=lax.Precision.HIGHEST
    )
    rows_adj = jnp.einsum(
        "sk,krc->src", pick_adj, all_pieces[:, 1], precision=lax.Precision.HIGHEST
    )
    rows = (rows_fwd + rows_adj).astype(jnp.bfloat16)
    return gathered_copies(rows, "term", 1)


def solution(mesh):
    placed = (
        P("sec", None, None),
        P("sec", "term", None, None),
        P("sec", "term", None, None),
        P("sec", "term"),
        P("sec"),
        P("sec"),
    )
    return jax.shard_map(
        local, mesh=mesh, in_specs=placed, out_specs=P("sec", None, None), check_vma=False
    )
```

profile of v0, /device:TPU:1, one launch (start us, length us, event | category | flops | bytes accessed | tf_op | source)
XLA Modules:
  0.0 217.1 jit_solution(3146875595708951832)
XLA Ops:
  6.5 0.7 all-gather.4.cloned.1.call-update
  8.6 60.7 %all-gather.4.cloned.1.call-done = bf16[16,512,512]{2,1,0:T(8,128)(2,1)} async-done(((bf16[1,512,512]{2,1,0:T(8,128)(2,1)}), bf16[16,512,512]{2,1,0:T(8,128)(2,1)}) %all-gather.4.cloned.1.call-update) | async-done | bytes 8388624 | tf_op jit(solution)/shard_map/all_gather | solution.py:48
  69.2 1.3 dynamic-slice_bitcast_fusion
  70.8 53.7 %while.12 = (s32[]{:T(128)}, f32[512,512]{1,0:T(8,128)S(1)}, f32[512,512]{1,0:T(8,128)S(1)}, s32[6]{0:T(128)S(1)}, s32[1,6]{1,0:T(1,128)S(1)}, /*index=5*/bf16[1...) while((s32[]{:T(128)}, f32[512,512]{1,0:T(8,128)S(1)}, ...), condition=%wide.region_3.4_spmd, body=%wide.region_0.3_spmd.sunk | while | flops 1074790400 | bytes 7342387 | solution.py:76
  70.8 0.7 dynamic_slice.44
  74.7 6.0 %conditional.2 = ((f32[512,512]{1,0:T(8,128)S(1)}, f32[512,512]{1,0:T(8,128)S(1)})) conditional(s32[]{:T(128)} %bitcast.55, (f32[512,512]{1,0:T(8,128)S(1)}, f32[512,512]{1,0:T(8,128)S(1)}) %tuple.30, (s32[]{:T(128)}, bf16[1,6,512,512]{3,2,1,0:T(8,128)(2,1)}, bf16[512,512]{1,0:T(8,128)(2,1)S(1)}, bf16[1,6,512,512]{3,2,1,0:T(8,128)(2,1)}, ...), branch_computations={%region_1.1_spmd, %region_2.2_spmd} | conditional | flops 1074790400 | bytes 7342138 | solution.py:74
  76.8 1.9 convolution_add_fusion
  78.8 1.9 convolution_add_fusion.1
  80.7 0.7 dynamic_slice.44
  84.7 6.0 %conditional.2 = ((f32[512,512]{1,0:T(8,128)S(1)}, f32[512,512]{1,0:T(8,128)S(1)})) conditional(s32[]{:T(128)} %bitcast.55, (f32[512,512]{1,0:T(8,128)S(1)}, f32[512,512]{1,0:T(8,128)S(1)}) %tuple.30, (s32[]{:T(128)}, bf16[1,6,512,512]{3,2,1,0:T(8,128)(2,1)}, bf16[512,512]{1,0:T(8,128)(2,1)S(1)}, bf16[1,6,512,512]{3,2,1,0:T(8,128)(2,1)}, ...), branch_computations={%region_1.1_spmd, %region_2.2_spmd} | conditional | flops 1074790400 | bytes 7342138 | solution.py:74
  86.7 1.9 convolution_add_fusion
  88.7 1.9 convolution_add_fusion.1
  94.6 6.0 %conditional.2 = ((f32[512,512]{1,0:T(8,128)S(1)}, f32[512,512]{1,0:T(8,128)S(1)})) conditional(s32[]{:T(128)} %bitcast.55, (f32[512,512]{1,0:T(8,128)S(1)}, f32[512,512]{1,0:T(8,128)S(1)}) %tuple.30, (s32[]{:T(128)}, bf16[1,6,512,512]{3,2,1,0:T(8,128)(2,1)}, bf16[512,512]{1,0:T(8,128)(2,1)S(1)}, bf16[1,6,512,512]{3,2,1,0:T(8,128)(2,1)}, ...), branch_computations={%region_1.1_spmd, %region_2.2_spmd} | conditional | flops 1074790400 | bytes 7342138 | solution.py:74
  96.7 2.0 convolution_add_fusion
  98.6 1.9 convolution_add_fusion.1
  108.6 6.0 %conditional.2 = ((f32[512,512]{1,0:T(8,128)S(1)}, f32[512,512]{1,0:T(8,128)S(1)})) conditional(s32[]{:T(128)} %bitcast.55, (f32[512,512]{1,0:T(8,128)S(1)}, f32[512,512]{1,0:T(8,128)S(1)}) %tuple.30, (s32[]{:T(128)}, bf16[1,6,512,512]{3,2,1,0:T(8,128)(2,1)}, bf16[512,512]{1,0:T(8,128)(2,1)S(1)}, bf16[1,6,512,512]{3,2,1,0:T(8,128)(2,1)}, ...), branch_computations={%region_1.1_spmd, %region_2.2_spmd} | conditional | flops 1074790400 | bytes 7342138 | solution.py:74
  110.6 1.9 convolution_add_fusion
  112.6 1.9 convolution_add_fusion.1
  118.5 6.0 %conditional.2 = ((f32[512,512]{1,0:T(8,128)S(1)}, f32[512,512]{1,0:T(8,128)S(1)})) conditional(s32[]{:T(128)} %bitcast.55, (f32[512,512]{1,0:T(8,128)S(1)}, f32[512,512]{1,0:T(8,128)S(1)}) %tuple.30, (s32[]{:T(128)}, bf16[1,6,512,512]{3,2,1,0:T(8,128)(2,1)}, bf16[512,512]{1,0:T(8,128)(2,1)S(1)}, bf16[1,6,512,512]{3,2,1,0:T(8,128)(2,1)}, ...), branch_computations={%region_1.1_spmd, %region_2.2_spmd} | conditional | flops 1074790400 | bytes 7342138 | solution.py:74
  120.6 1.9 convolution_add_fusion
  122.5 1.9 convolution_add_fusion.1
  124.6 1.1 maximum_bitcast_fusion
  125.7 6.3 %all-to-all-start = ((bf16[16,1,2,32,512]{4,3,2,1,0:T(8,128)(2,1)}), bf16[16,1,2,32,512]{4,3,2,1,0:T(8,128)(2,1)S(1)}, u32[]{:S(2)}, u32[]{:S(2)}) async-start(bf16[16,1,2,32,512]{4,3,2,1,0:T(8,128)(2,1)} %maximum_bitcast_fusion), calls=%async_computation | async-start | bytes 2097152 | tf_op jit(solution)/shard_map/all_to_all | solution.py:15
  132.0 16.1 %all-to-all-done = bf16[16,1,2,32,512]{4,3,2,1,0:T(8,128)(2,1)S(1)} async-done(((bf16[16,1,2,32,512]{4,3,2,1,0:T(8,128)(2,1)}), bf16[16,1,2,32,512]{4,3,2,1,0:T(8,128)(2,1)S(1)}, u32[]{:S(2)}, u32[]{:S(2)}) %all-to-all-start) | async-done | bytes 1048608 | tf_op jit(solution)/shard_map/all_to_all | solution.py:15
  148.6 0.7 copy-done
  149.3 37.2 %all-gather.6.cloned.1.call-done = f32[16,1,32770]{2,1,0:T(1,128)} async-done(((f32[1,1,32770]{2,1,0:T(1,128)}), f32[16,1,32770]{2,1,0:T(1,128)}) %all-gather.6.cloned.1.call-update) | async-done | bytes 2097296 | tf_op jit(solution)/shard_map/all_gather | solution.py:22
  186.5 1.7 copy.20
  188.4 1.2 copy.12
  190.1 1.1 fusion.18
  191.2 1.1 fusion.16
  192.3 17.1 %all_to_all.10 = bf16[16,1,32,512]{3,2,1,0:T(8,128)(2,1)S(1)} all-to-all(bf16[16,1,32,512]{3,2,1,0:T(8,128)(2,1)S(1)} %broadcast_in_dim.5), channel_id=1, replica_groups=mesh['sec'=16,'term'=16] {'term'}, dimensions={0} | all-to-all | bytes 1048576 | tf_op jit(solution)/shard_map/all_to_all | solution.py:38
  209.5 0.8 copy.39
  (32 shorter events, 7.9 us)
Async XLA Ops:
  6.5 64.2 %copy-start.1 = (s32[1,6]{1,0:T(1,128)S(1)}, s32[1,6]{1,0:T(1,128)}, u32[]{:S(2)}) copy-start(s32[1,6]{1,0:T(1,128)} %param.13) | copy-start | bytes 76
  6.5 62.7 %all-gather.4.cloned.1.call-start = ((), (), s32[]{:S(2)}) async-start(), calls=%async_computation.2 | async-start | bytes 8912896 | tf_op jit(solution)/shard_map/all_gather | solution.py:48
  125.7 22.4 %all-to-all-start = ((bf16[16,1,2,32,512]{4,3,2,1,0:T(8,128)(2,1)}), bf16[16,1,2,32,512]{4,3,2,1,0:T(8,128)(2,1)S(1)}, u32[]{:S(2)}, u32[]{:S(2)}) async-start(bf16[16,1,2,32,512]{4,3,2,1,0:T(8,128)(2,1)} %maximum_bitcast_fusion), calls=%async_computation | async-start | bytes 2097152 | tf_op jit(solution)/shard_map/all_to_all | solution.py:15
  132.0 54.5 %all-gather.6.cloned.1.call-start = ((), (), s32[]{:S(2)}) async-start(), calls=%async_computation.3 | async-start | bytes 2236928 | tf_op jit(solution)/shard_map/all_gather | solution.py:22
  148.6 0.7 copy-start
Sparse Core Ops, SparseCore 0:
  9.2 60.0 all-gather.3
  149.4 37.0 all-gather.5
where the time goes:
time: 218 us; the launch traced here: 217 us
  waiting for transfers between devices  115 us (53%)
  loops' own time  26.7 us (12%)
  matrix products  21.6 us (10%)
  blocking collectives  17.1 us (8%)
  between operations  14.9 us (7%)
  local copies, waits for them, and re-layouts  10.6 us (5%)
  starting transfers between devices  6.3 us (3%)
  other arithmetic  5.21 us (2%)
    all_gather x1, waiting for transfers between devices, local(): whole = lax.all_gather(psi, 'sec', axis=0, tiled=True)  60.7 us
    all_gather x1, waiting for transfers between devices, in_one_piece(): lax.all_gather(both, axis, axis=dim, tiled=True)  37.2 us
    all_to_all x1, blocking collectives, copy_for_each(): lax.all_to_all(jnp.broadcast_to(value[None], (peers, *value.shape)), axis...  17.1 us
    another operation x1, loops' own time, local(): lax.scan(term_step, (zero_block, zero_block), jnp.arange(local_terms, dty...  16.3 us
    all_to_all x1, waiting for transfers between devices, sent_and_summed(): lax.all_to_all(pieces, axis, split_axis=0, concat_axis=0, tiled=True)  16.1 us
    another operation x6, loops' own time, term_step(): lax.cond(term_mask[0, term] == 1, active, lambda carry: carry, acc)  10.4 us
    dot_general x5, matrix products, active(): jnp.dot(inner_adj, right, preferred_element_type=jnp.float32)  9.73 us
    dot_general x5, matrix products, active(): jnp.dot(inner_fwd, right.T, preferred_element_type=jnp.float32)  9.7 us
  transfers between devices with their start and end apart: 3, of which 3 were waited for; matrix products, arithmetic and copies ran while one was open for 0% of the time, Pallas kernels for 0%

commit v1 on v0

--- a/solution.py
+++ b/solution.py
@@ -45,7 +45,16 @@
 
 
 def local(psi, left_ops, right_ops, term_mask, pair_src, pair_dst):
-    whole = lax.all_gather(psi, "sec", axis=0, tiled=True)
+    ways = lax.axis_size("sec")
+    up = [(d, (d + 1) % ways) for d in range(ways)]
+    down = [(d, (d - 1) % ways) for d in range(ways)]
+    earlier, later = ([psi], [psi])
+    for _ in range(ways // 2):
+        earlier.append(lax.ppermute(earlier[-1], "sec", up))
+    for _ in range((ways - 1) // 2):
+        later.append(lax.ppermute(later[-1], "sec", down))
+    line = jnp.concatenate([*earlier[::-1], *later[1:]], axis=0)
+    whole = jnp.roll(line, (lax.axis_index("sec") - ways // 2) * psi.shape[0], axis=0)
     order = psi.shape[1]
     local_pairs = psi.shape[0]
     local_terms = left_ops.shape[1]

time: 218 us -> 254 us (1.17)
  starting transfers between devices: 6.3 us -> 54.2 us
  waiting for transfers between devices: 115 us -> 86.1 us
  local copies, waits for them, and re-layouts: 10.6 us -> 26.4 us
    all_gather x1 -> x0, waiting for transfers between devices: 60.7 us -> none  [local(): whole = lax.all_gather(psi, 'sec', axis=0, tiled=True)]
    ppermute x0 -> x15, starting transfers between devices: none -> 47.6 us  [the longest x7 33.2 us: local(): later.append(lax.ppermute(later[-1], 'sec', down))]
    ppermute x0 -> x15, waiting for transfers between devices: none -> 24.3 us  [the longest x8 15.2 us: local(): earlier.append(lax.ppermute(earlier[-1], 'sec', up))]
    unnamed x9 -> x62, local copies, waits for them, and re-layouts: 4.47 us -> 21.8 us
    all_gather x1, waiting for transfers between devices: 37.2 us -> 49.6 us  [in_one_piece(): lax.all_gather(both, axis, axis=dim, tiled=True)]
    all_to_all x1, waiting for transfers between devices: 16.1 us -> 12.1 us  [sent_and_summed(): lax.all_to_all(pieces, axis, split_axis=0, concat_axis=0, tiled=True)]
  transfers between devices with their start and end apart: 3 -> 17, of which waited for: 3 -> 13; matrix products, arithmetic and copies ran while one was open for 0% -> 4% of each run, Pallas kernels for 0% -> 0%
where the time goes in v1:
time: 254 us; the launch traced here: 252 us
  waiting for transfers between devices  86.1 us (34%)
  starting transfers between devices  54.2 us (21%)
  local copies, waits for them, and re-layouts  26.4 us (10%)
  loops' own time  25.8 us (10%)
  matrix products  21.6 us (9%)
  blocking collectives  17.1 us (7%)
  between operations  15.2 us (6%)
  other arithmetic  5.57 us (2%)
    all_gather x1, waiting for transfers between devices, in_one_piece(): lax.all_gather(both, axis, axis=dim, tiled=True)  49.6 us
    ppermute x7, starting transfers between devices, local(): later.append(lax.ppermute(later[-1], 'sec', down))  33.2 us
    unnamed x62, local copies, waits for them, and re-layouts  21.8 us
    all_to_all x1, blocking collectives, copy_for_each(): lax.all_to_all(jnp.broadcast_to(value[None], (peers, *value.shape)), axis...  17.1 us
    another operation x1, loops' own time, local(): lax.scan(term_step, (zero_block, zero_block), jnp.arange(local_terms, dty...  16 us
    ppermute x8, waiting for transfers between devices, local(): earlier.append(lax.ppermute(earlier[-1], 'sec', up))  15.2 us
    ppermute x8, starting transfers between devices, local(): earlier.append(lax.ppermute(earlier[-1], 'sec', up))  14.3 us
    all_to_all x1, waiting for transfers between devices, sent_and_summed(): lax.all_to_all(pieces, axis, split_axis=0, concat_axis=0, tiled=True)  12.1 us
  transfers between devices with their start and end apart: 17, of which 13 were waited for; matrix products, arithmetic and copies ran while one was open for 4% of the time, Pallas kernels for 0%

profile of v1, /device:TPU:1, one launch (start us, length us, event | category | flops | bytes accessed | tf_op | source)
XLA Modules:
  0.0 252.0 jit_solution(12631918597648687937)
XLA Ops:
  6.5 3.0 %collective-permute-start = (bf16[1,512,512]{2,1,0:T(8,128)(2,1)}, bf16[1,512,512]{2,1,0:T(8,128)(2,1)S(1)}, u32[]{:S(2)}, u32[]{:S(2)}) collective-permute-start(bf16[1,512,512]{2,1,0:T(8,128)(2,1)} %param.10), channel_id=1, source_target_pairs={{0,16},{16,32},{32,48},{48,64},{64,80},{80,96},{96,112},{112,128},... | collective-permute-start | bytes 1572872 | tf_op jit(solution)/shard_map/ppermute | solution.py:53
  9.6 6.4 %collective-permute-done = bf16[1,512,512]{2,1,0:T(8,128)(2,1)S(1)} collective-permute-done((bf16[1,512,512]{2,1,0:T(8,128)(2,1)}, bf16[1,512,512]{2,1,0:T(8,128)(2,1)S(1)}, u32[]{:S(2)}, u32[]{:S(2)}) %collective-permute-start) | collective-permute-done | bytes 524320 | tf_op jit(solution)/shard_map/ppermute | solution.py:53
  16.0 2.4 collective-permute-start.1
  18.4 2.1 collective-permute-start.8
  20.5 4.0 %collective-permute-done.1 = bf16[1,512,512]{2,1,0:T(8,128)(2,1)S(1)} collective-permute-done((bf16[1,512,512]{2,1,0:T(8,128)(2,1)S(1)}, bf16[1,512,512]{2,1,0:T(8,128)(2,1)S(1)}, u32[]{:S(2)}, u32[]{:S(2)}) %collective-permute-start.1) | collective-permute-done | bytes 524320 | tf_op jit(solution)/shard_map/ppermute | solution.py:53
  24.5 2.5 collective-permute-start.2
  27.5 3.0 %collective-permute-start.9 = (bf16[1,512,512]{2,1,0:T(8,128)(2,1)S(1)}, bf16[1,512,512]{2,1,0:T(8,128)(2,1)S(1)}, u32[]{:S(2)}, u32[]{:S(2)}) collective-permute-start(bf16[1,512,512]{2,1,0:T(8,128)(2,1)S(1)} %collective-permute-done.8), channel_id=1, source_target_pairs={{0,240},{16,0},{32,16},{48,32},{64,48},{80,64},{96,80},{112,96},{1... | collective-permute-start | bytes 1572872 | tf_op jit(solution)/shard_map/ppermute | solution.py:55
  30.4 2.7 %collective-permute-done.2 = bf16[1,512,512]{2,1,0:T(8,128)(2,1)S(1)} collective-permute-done((bf16[1,512,512]{2,1,0:T(8,128)(2,1)S(1)}, bf16[1,512,512]{2,1,0:T(8,128)(2,1)S(1)}, u32[]{:S(2)}, u32[]{:S(2)}) %collective-permute-start.2) | collective-permute-done | bytes 524320 | tf_op jit(solution)/shard_map/ppermute | solution.py:53
  33.1 2.5 collective-permute-start.3
  36.4 3.8 %collective-permute-start.10 = (bf16[1,512,512]{2,1,0:T(8,128)(2,1)S(1)}, bf16[1,512,512]{2,1,0:T(8,128)(2,1)S(1)}, u32[]{:S(2)}, u32[]{:S(2)}) collective-permute-start(bf16[1,512,512]{2,1,0:T(8,128)(2,1)S(1)} %collective-permute-done.9), channel_id=1, source_target_pairs={{0,240},{16,0},{32,16},{48,32},{64,48},{80,64},{96,80},{112,96},{1... | collective-permute-start | bytes 1572872 | tf_op jit(solution)/shard_map/ppermute | solution.py:55
  41.7 2.5 collective-permute-start.4
  46.1 4.7 %collective-permute-start.11 = (bf16[1,512,512]{2,1,0:T(8,128)(2,1)S(1)}, bf16[1,512,512]{2,1,0:T(8,128)(2,1)S(1)}, u32[]{:S(2)}, u32[]{:S(2)}) collective-permute-start(bf16[1,512,512]{2,1,0:T(8,128)(2,1)S(1)} %collective-permute-done.10), channel_id=1, source_target_pairs={{0,240},{16,0},{32,16},{48,32},{64,48},{80,64},{96,80},{112,96},{1... | collective-permute-start | bytes 1572872 | tf_op jit(solution)/shard_map/ppermute | solution.py:55
  52.8 2.2 collective-permute-done.11
  55.8 5.6 %collective-permute-start.12 = (bf16[1,512,512]{2,1,0:T(8,128)(2,1)S(1)}, bf16[1,512,512]{2,1,0:T(8,128)(2,1)}, u32[]{:S(2)}, u32[]{:S(2)}) collective-permute-start(bf16[1,512,512]{2,1,0:T(8,128)(2,1)S(1)} %collective-permute-done.11), channel_id=1, source_target_pairs={{0,240},{16,0},{32,16},{48,32},{64,48},{80,64},{96,80},{112,96},{1... | collective-permute-start | bytes 1572872 | tf_op jit(solution)/shard_map/ppermute | solution.py:55
  61.4 3.3 %collective-permute-done.12 = bf16[1,512,512]{2,1,0:T(8,128)(2,1)} collective-permute-done((bf16[1,512,512]{2,1,0:T(8,128)(2,1)S(1)}, bf16[1,512,512]{2,1,0:T(8,128)(2,1)}, u32[]{:S(2)}, u32[]{:S(2)}) %collective-permute-start.12) | collective-permute-done | bytes 524320 | tf_op jit(solution)/shard_map/ppermute | solution.py:55
  64.7 6.5 %collective-permute-start.13 = (bf16[1,512,512]{2,1,0:T(8,128)(2,1)}, bf16[1,512,512]{2,1,0:T(8,128)(2,1)}, u32[]{:S(2)}, u32[]{:S(2)}) collective-permute-start(bf16[1,512,512]{2,1,0:T(8,128)(2,1)} %collective-permute-done.12), channel_id=1, source_target_pairs={{0,240},{16,0},{32,16},{48,32},{64,48},{80,64},{96,80},{112,96},{1... | collective-permute-start | bytes 1572872 | tf_op jit(solution)/shard_map/ppermute | solution.py:55
  73.9 7.5 %collective-permute-start.14 = (bf16[1,512,512]{2,1,0:T(8,128)(2,1)}, bf16[1,512,512]{2,1,0:T(8,128)(2,1)S(1)}, u32[]{:S(2)}, u32[]{:S(2)}) collective-permute-start(bf16[1,512,512]{2,1,0:T(8,128)(2,1)} %collective-permute-done.13), channel_id=1, source_target_pairs={{0,240},{16,0},{32,16},{48,32},{64,48},{80,64},{96,80},{112,96},{1... | collective-permute-start | bytes 1572872 | tf_op jit(solution)/shard_map/ppermute | solution.py:55
  97.9 52.8 %while.12 = (s32[]{:T(128)}, f32[512,512]{1,0:T(8,128)S(1)}, f32[512,512]{1,0:T(8,128)S(1)}, s32[6]{0:T(128)S(1)}, s32[1,6]{1,0:T(1,128)S(1)}, /*index=5*/bf16[1...) while((s32[]{:T(128)}, f32[512,512]{1,0:T(8,128)S(1)}, ...), condition=%wide.region_3.4_spmd, body=%wide.region_0.3_spmd.sunk | while | flops 1074790400 | bytes 7342387 | solution.py:85
  101.8 5.9 %conditional.2 = ((f32[512,512]{1,0:T(8,128)S(1)}, f32[512,512]{1,0:T(8,128)S(1)})) conditional(s32[]{:T(128)} %bitcast.55, (f32[512,512]{1,0:T(8,128)S(1)}, f32[512,512]{1,0:T(8,128)S(1)}) %tuple.30, (s32[]{:T(128)}, bf16[1,6,512,512]{3,2,1,0:T(8,128)(2,1)}, bf16[512,512]{1,0:T(8,128)(2,1)S(1)}, bf16[1,6,512,512]{3,2,1,0:T(8,128)(2,1)}, ...), branch_computations={%region_1.1_spmd, %region_2.2_spmd} | conditional | flops 1074790400 | bytes 7342138 | solution.py:83
  103.7 1.9 convolution_add_fusion
  111.5 5.9 %conditional.2 = ((f32[512,512]{1,0:T(8,128)S(1)}, f32[512,512]{1,0:T(8,128)S(1)})) conditional(s32[]{:T(128)} %bitcast.55, (f32[512,512]{1,0:T(8,128)S(1)}, f32[512,512]{1,0:T(8,128)S(1)}) %tuple.30, (s32[]{:T(128)}, bf16[1,6,512,512]{3,2,1,0:T(8,128)(2,1)}, bf16[512,512]{1,0:T(8,128)(2,1)S(1)}, bf16[1,6,512,512]{3,2,1,0:T(8,128)(2,1)}, ...), branch_computations={%region_1.1_spmd, %region_2.2_spmd} | conditional | flops 1074790400 | bytes 7342138 | solution.py:83
  113.5 1.9 convolution_add_fusion
  121.3 5.9 %conditional.2 = ((f32[512,512]{1,0:T(8,128)S(1)}, f32[512,512]{1,0:T(8,128)S(1)})) conditional(s32[]{:T(128)} %bitcast.55, (f32[512,512]{1,0:T(8,128)S(1)}, f32[512,512]{1,0:T(8,128)S(1)}) %tuple.30, (s32[]{:T(128)}, bf16[1,6,512,512]{3,2,1,0:T(8,128)(2,1)}, bf16[512,512]{1,0:T(8,128)(2,1)S(1)}, bf16[1,6,512,512]{3,2,1,0:T(8,128)(2,1)}, ...), branch_computations={%region_1.1_spmd, %region_2.2_spmd} | conditional | flops 1074790400 | bytes 7342138 | solution.py:83
  123.3 1.9 convolution_add_fusion
  135.0 5.9 %conditional.2 = ((f32[512,512]{1,0:T(8,128)S(1)}, f32[512,512]{1,0:T(8,128)S(1)})) conditional(s32[]{:T(128)} %bitcast.55, (f32[512,512]{1,0:T(8,128)S(1)}, f32[512,512]{1,0:T(8,128)S(1)}) %tuple.30, (s32[]{:T(128)}, bf16[1,6,512,512]{3,2,1,0:T(8,128)(2,1)}, bf16[512,512]{1,0:T(8,128)(2,1)S(1)}, bf16[1,6,512,512]{3,2,1,0:T(8,128)(2,1)}, ...), branch_computations={%region_1.1_spmd, %region_2.2_spmd} | conditional | flops 1074790400 | bytes 7342138 | solution.py:83
  137.0 1.9 convolution_add_fusion
  144.8 5.9 %conditional.2 = ((f32[512,512]{1,0:T(8,128)S(1)}, f32[512,512]{1,0:T(8,128)S(1)})) conditional(s32[]{:T(128)} %bitcast.55, (f32[512,512]{1,0:T(8,128)S(1)}, f32[512,512]{1,0:T(8,128)S(1)}) %tuple.30, (s32[]{:T(128)}, bf16[1,6,512,512]{3,2,1,0:T(8,128)(2,1)}, bf16[512,512]{1,0:T(8,128)(2,1)S(1)}, bf16[1,6,512,512]{3,2,1,0:T(8,128)(2,1)}, ...), branch_computations={%region_1.1_spmd, %region_2.2_spmd} | conditional | flops 1074790400 | bytes 7342138 | solution.py:83
  146.8 1.9 convolution_add_fusion
  151.9 6.6 %all-to-all-start = ((bf16[16,1,2,32,512]{4,3,2,1,0:T(8,128)(2,1)}), bf16[16,1,2,32,512]{4,3,2,1,0:T(8,128)(2,1)S(1)}, u32[]{:S(2)}, u32[]{:S(2)}) async-start(bf16[16,1,2,32,512]{4,3,2,1,0:T(8,128)(2,1)} %maximum_bitcast_fusion), calls=%async_computation | async-start | bytes 2097152 | tf_op jit(solution)/shard_map/all_to_all | solution.py:15
  158.5 12.1 %all-to-all-done = bf16[16,1,2,32,512]{4,3,2,1,0:T(8,128)(2,1)S(1)} async-done(((bf16[16,1,2,32,512]{4,3,2,1,0:T(8,128)(2,1)}), bf16[16,1,2,32,512]{4,3,2,1,0:T(8,128)(2,1)S(1)}, u32[]{:S(2)}, u32[]{:S(2)}) %all-to-all-start) | async-done | bytes 1048608 | tf_op jit(solution)/shard_map/all_to_all | solution.py:15
  171.9 49.6 %all-gather.3.cloned.1.call-done = f32[16,1,32770]{2,1,0:T(1,128)} async-done(((f32[1,1,32770]{2,1,0:T(1,128)}), f32[16,1,32770]{2,1,0:T(1,128)}) %all-gather.3.cloned.1.call-update) | async-done | bytes 2097296 | tf_op jit(solution)/shard_map/all_gather | solution.py:22
  227.3 17.1 %all_to_all.10 = bf16[16,1,32,512]{3,2,1,0:T(8,128)(2,1)S(1)} all-to-all(bf16[16,1,32,512]{3,2,1,0:T(8,128)(2,1)S(1)} %broadcast_in_dim.5), channel_id=1, replica_groups=mesh['sec'=16,'term'=16] {'term'}, dimensions={0} | all-to-all | bytes 1048576 | tf_op jit(solution)/shard_map/all_to_all | solution.py:38
  (113 shorter events, 51.1 us)
Async XLA Ops:
  6.5 88.5 %copy-start = (bf16[1,512,512]{2,1,0:T(8,128)(2,1)S(1)}, bf16[1,512,512]{2,1,0:T(8,128)(2,1)}, u32[]{:S(2)}) copy-start(bf16[1,512,512]{2,1,0:T(8,128)(2,1)} %param.10) | copy-start | bytes 1572868
  6.5 9.5 %collective-permute-start = (bf16[1,512,512]{2,1,0:T(8,128)(2,1)}, bf16[1,512,512]{2,1,0:T(8,128)(2,1)S(1)}, u32[]{:S(2)}, u32[]{:S(2)}) collective-permute-start(bf16[1,512,512]{2,1,0:T(8,128)(2,1)} %param.10), channel_id=1, source_target_pairs={{0,16},{16,32},{32,48},{48,64},{64,80},{80,96},{96,112},{112,128},... | collective-permute-start | bytes 1572872 | tf_op jit(solution)/shard_map/ppermute | solution.py:53
  16.0 8.5 %collective-permute-start.1 = (bf16[1,512,512]{2,1,0:T(8,128)(2,1)S(1)}, bf16[1,512,512]{2,1,0:T(8,128)(2,1)S(1)}, u32[]{:S(2)}, u32[]{:S(2)}) collective-permute-start(bf16[1,512,512]{2,1,0:T(8,128)(2,1)S(1)} %collective-permute-done), channel_id=1, source_target_pairs={{0,16},{16,32},{32,48},{48,64},{64,80},{80,96},{96,112},{112,128},... | collective-permute-start | bytes 1572872 | tf_op jit(solution)/shard_map/ppermute | solution.py:53
  18.4 9.1 %collective-permute-start.8 = (bf16[1,512,512]{2,1,0:T(8,128)(2,1)}, bf16[1,512,512]{2,1,0:T(8,128)(2,1)S(1)}, u32[]{:S(2)}, u32[]{:S(2)}) collective-permute-start(bf16[1,512,512]{2,1,0:T(8,128)(2,1)} %param.10), channel_id=1, source_target_pairs={{0,240},{16,0},{32,16},{48,32},{64,48},{80,64},{96,80},{112,96},{1... | collective-permute-start | bytes 1572872 | tf_op jit(solution)/shard_map/ppermute | solution.py:55
  24.5 8.6 %collective-permute-start.2 = (bf16[1,512,512]{2,1,0:T(8,128)(2,1)S(1)}, bf16[1,512,512]{2,1,0:T(8,128)(2,1)S(1)}, u32[]{:S(2)}, u32[]{:S(2)}) collective-permute-start(bf16[1,512,512]{2,1,0:T(8,128)(2,1)S(1)} %collective-permute-done.1), channel_id=1, source_target_pairs={{0,16},{16,32},{32,48},{48,64},{64,80},{80,96},{96,112},{112,128},... | collective-permute-start | bytes 1572872 | tf_op jit(solution)/shard_map/ppermute | solution.py:53
  27.5 8.9 %collective-permute-start.9 = (bf16[1,512,512]{2,1,0:T(8,128)(2,1)S(1)}, bf16[1,512,512]{2,1,0:T(8,128)(2,1)S(1)}, u32[]{:S(2)}, u32[]{:S(2)}) collective-permute-start(bf16[1,512,512]{2,1,0:T(8,128)(2,1)S(1)} %collective-permute-done.8), channel_id=1, source_target_pairs={{0,240},{16,0},{32,16},{48,32},{64,48},{80,64},{96,80},{112,96},{1... | collective-permute-start | bytes 1572872 | tf_op jit(solution)/shard_map/ppermute | solution.py:55
  33.1 8.6 %collective-permute-start.3 = (bf16[1,512,512]{2,1,0:T(8,128)(2,1)S(1)}, bf16[1,512,512]{2,1,0:T(8,128)(2,1)S(1)}, u32[]{:S(2)}, u32[]{:S(2)}) collective-permute-start(bf16[1,512,512]{2,1,0:T(8,128)(2,1)S(1)} %collective-permute-done.2), channel_id=1, source_target_pairs={{0,16},{16,32},{32,48},{48,64},{64,80},{80,96},{96,112},{112,128},... | collective-permute-start | bytes 1572872 | tf_op jit(solution)/shard_map/ppermute | solution.py:53
  36.4 8.9 %collective-permute-start.10 = (bf16[1,512,512]{2,1,0:T(8,128)(2,1)S(1)}, bf16[1,512,512]{2,1,0:T(8,128)(2,1)S(1)}, u32[]{:S(2)}, u32[]{:S(2)}) collective-permute-start(bf16[1,512,512]{2,1,0:T(8,128)(2,1)S(1)} %collective-permute-done.9), channel_id=1, source_target_pairs={{0,240},{16,0},{32,16},{48,32},{64,48},{80,64},{96,80},{112,96},{1... | collective-permute-start | bytes 1572872 | tf_op jit(solution)/shard_map/ppermute | solution.py:55
  41.7 23.0 %copy-start.5 = (bf16[1,512,512]{2,1,0:T(8,128)(2,1)}, bf16[1,512,512]{2,1,0:T(8,128)(2,1)S(1)}, u32[]{:S(2)}) copy-start(bf16[1,512,512]{2,1,0:T(8,128)(2,1)S(1)} %collective-permute-done.3) | copy-start | bytes 1572868
  41.7 9.6 %collective-permute-start.4 = (bf16[1,512,512]{2,1,0:T(8,128)(2,1)S(1)}, bf16[1,512,512]{2,1,0:T(8,128)(2,1)S(1)}, u32[]{:S(2)}, u32[]{:S(2)}) collective-permute-start(bf16[1,512,512]{2,1,0:T(8,128)(2,1)S(1)} %collective-permute-done.3), channel_id=1, source_target_pairs={{0,16},{16,32},{32,48},{48,64},{64,80},{80,96},{96,112},{112,128},... | collective-permute-start | bytes 1572872 | tf_op jit(solution)/shard_map/ppermute | solution.py:53
  45.3 0.8 copy-start.1
  46.1 8.9 %collective-permute-start.11 = (bf16[1,512,512]{2,1,0:T(8,128)(2,1)S(1)}, bf16[1,512,512]{2,1,0:T(8,128)(2,1)S(1)}, u32[]{:S(2)}, u32[]{:S(2)}) collective-permute-start(bf16[1,512,512]{2,1,0:T(8,128)(2,1)S(1)} %collective-permute-done.10), channel_id=1, source_target_pairs={{0,240},{16,0},{32,16},{48,32},{64,48},{80,64},{96,80},{112,96},{1... | collective-permute-start | bytes 1572872 | tf_op jit(solution)/shard_map/ppermute | solution.py:55
  51.3 19.9 %copy-start.7 = (bf16[1,512,512]{2,1,0:T(8,128)(2,1)}, bf16[1,512,512]{2,1,0:T(8,128)(2,1)S(1)}, u32[]{:S(2)}) copy-start(bf16[1,512,512]{2,1,0:T(8,128)(2,1)S(1)} %collective-permute-done.4) | copy-start | bytes 1572868
  51.3 10.1 %collective-permute-start.5 = (bf16[1,512,512]{2,1,0:T(8,128)(2,1)S(1)}, bf16[1,512,512]{2,1,0:T(8,128)(2,1)S(1)}, u32[]{:S(2)}, u32[]{:S(2)}) collective-permute-start(bf16[1,512,512]{2,1,0:T(8,128)(2,1)S(1)} %collective-permute-done.4), channel_id=1, source_target_pairs={{0,16},{16,32},{32,48},{48,64},{64,80},{80,96},{96,112},{112,128},... | collective-permute-start | bytes 1572872 | tf_op jit(solution)/shard_map/ppermute | solution.py:53
  55.0 0.8 copy-start.3
  55.8 8.9 %collective-permute-start.12 = (bf16[1,512,512]{2,1,0:T(8,128)(2,1)S(1)}, bf16[1,512,512]{2,1,0:T(8,128)(2,1)}, u32[]{:S(2)}, u32[]{:S(2)}) collective-permute-start(bf16[1,512,512]{2,1,0:T(8,128)(2,1)S(1)} %collective-permute-done.11), channel_id=1, source_target_pairs={{0,240},{16,0},{32,16},{48,32},{64,48},{80,64},{96,80},{112,96},{1... | collective-permute-start | bytes 1572872 | tf_op jit(solution)/shard_map/ppermute | solution.py:55
  61.4 9.8 %copy-start.9 = (bf16[1,512,512]{2,1,0:T(8,128)(2,1)}, bf16[1,512,512]{2,1,0:T(8,128)(2,1)S(1)}, u32[]{:S(2)}) copy-start(bf16[1,512,512]{2,1,0:T(8,128)(2,1)S(1)} %collective-permute-done.5) | copy-start | bytes 1572868
  61.4 9.8 %collective-permute-start.6 = (bf16[1,512,512]{2,1,0:T(8,128)(2,1)S(1)}, bf16[1,512,512]{2,1,0:T(8,128)(2,1)}, u32[]{:S(2)}, u32[]{:S(2)}) collective-permute-start(bf16[1,512,512]{2,1,0:T(8,128)(2,1)S(1)} %collective-permute-done.5), channel_id=1, source_target_pairs={{0,16},{16,32},{32,48},{48,64},{64,80},{80,96},{96,112},{112,128},... | collective-permute-start | bytes 1572872 | tf_op jit(solution)/shard_map/ppermute | solution.py:53
  64.7 9.2 %collective-permute-start.13 = (bf16[1,512,512]{2,1,0:T(8,128)(2,1)}, bf16[1,512,512]{2,1,0:T(8,128)(2,1)}, u32[]{:S(2)}, u32[]{:S(2)}) collective-permute-start(bf16[1,512,512]{2,1,0:T(8,128)(2,1)} %collective-permute-done.12), channel_id=1, source_target_pairs={{0,240},{16,0},{32,16},{48,32},{64,48},{80,64},{96,80},{112,96},{1... | collective-permute-start | bytes 1572872 | tf_op jit(solution)/shard_map/ppermute | solution.py:55
  71.3 10.2 %collective-permute-start.7 = (bf16[1,512,512]{2,1,0:T(8,128)(2,1)}, bf16[1,512,512]{2,1,0:T(8,128)(2,1)}, u32[]{:S(2)}, u32[]{:S(2)}) collective-permute-start(bf16[1,512,512]{2,1,0:T(8,128)(2,1)} %collective-permute-done.6), channel_id=1, source_target_pairs={{0,16},{16,32},{32,48},{48,64},{64,80},{80,96},{96,112},{112,128},... | collective-permute-start | bytes 1572872 | tf_op jit(solution)/shard_map/ppermute | solution.py:53
  72.6 22.1 %copy-start.10 = (bf16[1,512,512]{2,1,0:T(8,128)(2,1)S(1)}, bf16[1,512,512]{2,1,0:T(8,128)(2,1)}, u32[]{:S(2)}) copy-start(bf16[1,512,512]{2,1,0:T(8,128)(2,1)} %copy-done.9) | copy-start | bytes 1572868
  72.6 22.2 %copy-start.8 = (bf16[1,512,512]{2,1,0:T(8,128)(2,1)S(1)}, bf16[1,512,512]{2,1,0:T(8,128)(2,1)}, u32[]{:S(2)}) copy-start(bf16[1,512,512]{2,1,0:T(8,128)(2,1)} %copy-done.7) | copy-start | bytes 1572868
  72.6 22.2 %copy-start.6 = (bf16[1,512,512]{2,1,0:T(8,128)(2,1)S(1)}, bf16[1,512,512]{2,1,0:T(8,128)(2,1)}, u32[]{:S(2)}) copy-start(bf16[1,512,512]{2,1,0:T(8,128)(2,1)} %copy-done.5) | copy-start | bytes 1572868
  72.6 22.5 %copy-start.2 = (bf16[1,512,512]{2,1,0:T(8,128)(2,1)S(1)}, bf16[1,512,512]{2,1,0:T(8,128)(2,1)}, u32[]{:S(2)}) copy-start(bf16[1,512,512]{2,1,0:T(8,128)(2,1)} %copy-done.1) | copy-start | bytes 1572868
  72.7 22.6 %copy-start.4 = (bf16[1,512,512]{2,1,0:T(8,128)(2,1)S(1)}, bf16[1,512,512]{2,1,0:T(8,128)(2,1)}, u32[]{:S(2)}) copy-start(bf16[1,512,512]{2,1,0:T(8,128)(2,1)} %copy-done.3) | copy-start | bytes 1572868
  73.9 18.6 %collective-permute-start.14 = (bf16[1,512,512]{2,1,0:T(8,128)(2,1)}, bf16[1,512,512]{2,1,0:T(8,128)(2,1)S(1)}, u32[]{:S(2)}, u32[]{:S(2)}) collective-permute-start(bf16[1,512,512]{2,1,0:T(8,128)(2,1)} %collective-permute-done.13), channel_id=1, source_target_pairs={{0,240},{16,0},{32,16},{48,32},{64,48},{80,64},{96,80},{112,96},{1... | collective-permute-start | bytes 1572872 | tf_op jit(solution)/shard_map/ppermute | solution.py:55
  85.8 12.0 %copy-start.12 = (s32[1,6]{1,0:T(1,128)S(1)}, s32[1,6]{1,0:T(1,128)}, u32[]{:S(2)}) copy-start(s32[1,6]{1,0:T(1,128)} %param.13) | copy-start | bytes 76
  151.9 18.8 %all-to-all-start = ((bf16[16,1,2,32,512]{4,3,2,1,0:T(8,128)(2,1)}), bf16[16,1,2,32,512]{4,3,2,1,0:T(8,128)(2,1)S(1)}, u32[]{:S(2)}, u32[]{:S(2)}) async-start(bf16[16,1,2,32,512]{4,3,2,1,0:T(8,128)(2,1)} %maximum_bitcast_fusion), calls=%async_computation | async-start | bytes 2097152 | tf_op jit(solution)/shard_map/all_to_all | solution.py:15
  158.5 63.0 %all-gather.3.cloned.1.call-start = ((), (), s32[]{:S(2)}) async-start(), calls=%async_computation.2 | async-start | bytes 2236928 | tf_op jit(solution)/shard_map/all_gather | solution.py:22
  171.2 0.7 copy-start.11
Sparse Core Ops, SparseCore 0:
  172.0 49.4 all-gather.2
